TPU v7x, 128 devices: a whole 4x4x4 slice. The times are simulated.
128 devices in a mesh: orow: 16 (over z, x), ocol: 8 (over y, core).
Axes of the slice: x: 4, y: 4, z: 4, core: 2. Of those that a mesh axis runs over, the one named last changes fastest.
Arguments:
- integrals: bfloat16 [2304, 32, 384], P('ocol', 'orow'), may hold values from -0.29882812 to 0.29882812
- occ_count: int32 [16], replicated, may hold values from 1 to 2
- occ_energy: float32 [32], replicated, may hold values from -2 to -0.5
- vir_energy: float32 [384], replicated, may hold values from 0.3 to 2.5
- task_iblock: int32 [64, 1], replicated, may hold values from 0 to 15; in each aligned block of 64 rows (0 to 63, 64 to 127, ...) at most 8 rows name the same one
- task_jblock: int32 [64], replicated, may hold values from 0 to 15
Outputs:
- gamma_out: float32 [2304, 32, 384], P('ocol', 'orow')
- density: float32 [384, 384], replicated
Inputs may be any that keep to these rules, and one draw needn't show every extreme that they name: `task_iblock`: no first block is named by more than 8 tasks, and some first block by exactly 8.
All inputs are finite; a program needn't handle non-finite values.
Results may differ from a plain program's by a relative error of at most 0.0019.
Values may be sent and summed in bfloat16 or wider, within the bound.
No kernel may reach another device: no remote copies, remote signals or barrier semaphores. Data moves between devices by JAX's collectives and lax.ppermute only.
A program may use at most 128 MiB of HBM per device.

v0:
```python
import jax
import jax.numpy as jnp
from jax import lax
from jax.sharding import Mesh
from jax.sharding import PartitionSpec as P

OROW = ("orow_0", "orow_1")
OCOL = ("ocol_0", "ocol_1")
OROW_OCOL = ("orow_0", "orow_1", "ocol_0", "ocol_1")


def rows_for(lines, length):
    spare = -lines.shape[0] % length
    if not spare:
        return lines
    return jnp.concatenate([lines, jnp.zeros((spare, *lines.shape[1:]), lines.dtype)])


def sum_in_order(pieces, axes, turns):
    lengths = [lax.axis_size(a) for a in axes]
    pieces = pieces.reshape(*lengths, *pieces.shape[1:])
    pieces = pieces.transpose(*turns, *range(len(axes), pieces.ndim))
    pieces = pieces.reshape(-1, *pieces.shape[len(axes) :])
    for k in turns:
        pieces = lax.psum_scatter(pieces, axes[k], scatter_dimension=0, tiled=True)
    return pieces[0]


def gather_in_order(x, axes, turns):
    pieces = x
    for k in turns:
        pieces = lax.all_gather(pieces, axes[k])
    done = turns[::-1]
    back = [done.index(k) for k in range(len(axes))]
    pieces = pieces.transpose(*back, *range(len(axes), pieces.ndim))
    return pieces.reshape(-1, *x.shape)


def total_of(x, axes, turns):
    length, lines = (lax.axis_size(axes), x.reshape(-1, *x.shape[1:][-1:]))
    pieces = rows_for(lines, length).reshape(length, -1, *lines.shape[1:])
    own = sum_in_order(pieces, axes, turns)
    whole = gather_in_order(own, axes, turns[::-1]).reshape(-1, *lines.shape[1:])
    return whole[: len(lines)].reshape(x.shape)


def make_amplitudes(k_total, i_energy, j_energy, vir_energy, usable):
    slots = k_total.shape[0]
    orbitals = i_energy.shape[1]
    virtuals = vir_energy.shape[0]
    k_grid = k_total.reshape(slots, orbitals, virtuals, orbitals, virtuals)
    denominator = (
        i_energy[:, :, None, None, None]
        + j_energy[:, None, None, :, None]
        - vir_energy[None, None, :, None, None]
        - vir_energy[None, None, None, None, :]
    )
    values = (2.0 * k_grid - jnp.swapaxes(k_grid, 2, 4)) / denominator
    values = values * usable[:, None, None, None, None]
    return values.astype(jnp.bfloat16).reshape(slots, orbitals * virtuals, orbitals * virtuals)


def local(integrals, occ_count, occ_energy, vir_energy, task_iblock, task_jblock):
    aux_local = integrals.shape[0]
    orbitals = integrals.shape[1]
    virtuals = integrals.shape[2]
    span = orbitals * virtuals
    block_total = lax.axis_size(OROW)
    col_total = lax.axis_size(OCOL)
    my_row = lax.axis_index(OROW)
    my_col = lax.axis_index(OCOL)
    active = jnp.arange(orbitals) < occ_count[my_row]
    masked = integrals * active.astype(jnp.bfloat16)[None, :, None]
    gathered = lax.all_gather(masked, OROW, axis=1, tiled=True)
    flat_blocks = gathered.reshape(aux_local, block_total, span)
    first_list = task_iblock[:, 0]
    task_total = first_list.shape[0]
    per_row = task_total // block_total
    task_ids = my_row * per_row + jnp.arange(per_row)
    i_block = first_list[task_ids]
    j_block = task_jblock[task_ids]
    usable = jnp.ones((per_row,), jnp.float32)
    energy_grid = occ_energy.reshape(block_total, orbitals)
    i_rows = jnp.take(flat_blocks, i_block, axis=1)
    j_rows = jnp.take(flat_blocks, j_block, axis=1)
    k_partial = jnp.einsum("psx,psy->sxy", i_rows, j_rows, preferred_element_type=jnp.float32)
    slots = k_partial.shape[0]
    i_energy = energy_grid[i_block]
    j_energy = energy_grid[j_block]
    k_total = lax.psum(k_partial, OCOL)
    amplitudes = make_amplitudes(k_total, i_energy, j_energy, vir_energy, usable)
    gamma_i = jnp.einsum("sxy,psy->psx", amplitudes, j_rows, preferred_element_type=jnp.float32)
    gamma_j = jnp.einsum("sxy,psx->psy", amplitudes, i_rows, preferred_element_type=jnp.float32)
    slice_width = span // col_total
    amp_grid = amplitudes.reshape(slots, orbitals, virtuals, span)
    column_part = lax.dynamic_slice_in_dim(amp_grid, my_col * slice_width, slice_width, 3)
    dens_part = jnp.einsum(
        "siaw,sibw->ab", column_part, column_part, preferred_element_type=jnp.float32
    )
    block_ids = jnp.arange(block_total)
    i_onehot = (i_block[:, None] == block_ids[None, :]).astype(jnp.float32)
    j_onehot = (j_block[:, None] == block_ids[None, :]).astype(jnp.float32)
    buffer = jnp.einsum(
        "sk,psx->pkx", i_onehot, gamma_i, precision=lax.Precision.HIGHEST
    ) + jnp.einsum("sk,psx->pkx", j_onehot, gamma_j, precision=lax.Precision.HIGHEST)
    owned = lax.psum_scatter(buffer, OROW, scatter_dimension=1, tiled=True)
    gamma_out = owned.reshape(aux_local, orbitals, virtuals)
    density = total_of(dens_part, OROW_OCOL, (0, 1, 2, 3)) / task_total
    return (gamma_out, density)


def solution(mesh):
    finer = Mesh(mesh.devices.reshape(4, 4, 4, 2), ("orow_0", "orow_1", "ocol_0", "ocol_1"))
    placed = (P(OCOL, OROW, None), P(), P(), P(), P(), P())
    return jax.shard_map(
        local, mesh=finer, in_specs=placed, out_specs=(P(OCOL, OROW, None), P()), check_vma=False
    )
```

profile of v0, /device:TPU:1, one launch (start us, length us, event | category | flops | bytes accessed | tf_op | source)
XLA Modules:
  0.0 520.0 jit_solution(48696897312067520)
XLA Ops:
  7.2 0.0 all-gather.5.cloned.1.call-start
  7.2 1.2 dynamic_slice.6
  8.5 0.6 compare_convert_fusion
  9.1 1.9 copy_multiply_fusion.1
  11.0 0.0 all-gather.5.cloned.1.call-update
  11.0 0.0 all-reduce.9.cloned.1.call-start
  11.1 0.6 gather_fusion.1
  11.8 1.3 gather_fusion
  13.1 66.1 %all-gather.5.cloned.1.call-done = bf16[288,32,384]{2,0,1:T(8,128)(2,1)} async-done(((bf16[288,2,384]{2,0,1:T(8,128)(2,1)}), bf16[288,32,384]{2,0,1:T(8,128)(2,1)}) %all-gather.5.cloned.1.call-update) | async-done | bytes 7077904 | tf_op jit(solution)/shard_map/all_gather | solution.py:74
  79.2 8.5 %copy.47 = bf16[288,32,384]{2,1,0:T(8,128)(2,1)} copy(bf16[288,32,384]{2,0,1:T(8,128)(2,1)} %all-gather.5.cloned.1.call-done) | data formatting | bytes 14155776 | tf_op jit(solution)/shard_map/all_gather | solution.py:74
  87.8 11.3 %reshape.91 = bf16[288,16,768]{2,1,0:T(8,128)(2,1)} reshape(bf16[288,32,384]{2,1,0:T(8,128)(2,1)} %copy.47) | data formatting | bytes 14155776 | tf_op jit(solution)/shard_map/reshape | solution.py:75
  99.1 8.3 %copy.48 = bf16[288,16,768]{2,0,1:T(8,128)(2,1)} copy(bf16[288,16,768]{2,1,0:T(8,128)(2,1)} %reshape.91) | data formatting | bytes 14155776 | tf_op jit(solution)/shard_map/reshape | solution.py:75
  107.4 3.7 gather_fusion.5
  111.1 3.7 gather_fusion.4
  114.8 5.2 fusion.6
  120.0 12.5 %reshape.92 = f32[4,2,384,2,384]{4,3,2,1,0:T(2,128)} reshape(f32[4,768,768]{2,1,0:T(8,128)} %fusion.6) | data formatting | bytes 18874368 | tf_op jit(solution)/shard_map/reshape | solution.py:51
  132.5 14.8 %copy.50 = f32[4,2,384,2,384]{2,4,3,1,0:T(8,128)} copy(f32[4,2,384,2,384]{4,3,2,1,0:T(2,128)} %reshape.92) | data formatting | bytes 18874368 | tf_op jit(solution)/shard_map/reshape | solution.py:51
  147.3 0.5 all-reduce.11.cloned.1.call-start
  147.9 0.7 reshape.93
  148.6 0.7 fusion.19
  149.3 0.6 pad_clamp_fusion
  149.9 1.3 gather_fusion.3
  151.1 0.6 fusion.18
  151.7 0.6 pad_clamp_fusion.1
  152.3 1.3 gather_fusion.2
  153.6 1.2 dynamic-slice.2
  155.5 0.8 broadcast_add_fusion
  156.2 1.4 broadcast_subtract_fusion
  157.6 103.2 %all-reduce.9.cloned.1.call-done = f32[4,2,384,2,384]{2,4,3,1,0:T(8,128)} async-done(((f32[4,2,384,2,384]{2,4,3,1,0:T(8,128)}), f32[4,2,384,2,384]{2,4,3,1,0:T(8,128)}) %all-reduce.9.cloned.1.call-update) | async-done | bytes 9437200 | tf_op jit(solution)/shard_map/psum | solution.py:90
  260.8 9.6 %copy.51 = f32[4,2,384,2,384]{4,2,3,1,0:T(8,128)} copy(f32[4,2,384,2,384]{2,4,3,1,0:T(8,128)} %all-reduce.9.cloned.1.call-done) | data formatting | bytes 18874368 | tf_op jit(solution)/shard_map/psum | solution.py:90
  270.4 9.6 %fusion.1 = bf16[4,2,384,2,384]{4,2,3,1,0:T(8,128)(2,1)} fusion(f32[4,2,384,2,384]{2,4,3,1,0:T(8,128)} %all-reduce.9.cloned.1.call-done, f32[4,2,384,2,384]{4,2,3,1,0:T(8,128)} %copy.51, f32[384]{0:T(512)S(1)} %copy-done.2, f32[4,2,384,2]{2,3,1,0:T(2,128)} %broadcast_subtract_fusion), kind=kLoop, calls=%fused_computation.9 | loop fusion | flops 11796480 | bytes 23619072 | tf_op jit(solution)/shard_map/convert_element_type | solution.py:60
  280.0 6.7 %copy.63 = bf16[4,2,384,2,384]{2,4,3,0,1:T(8,128)(2,1)} copy(bf16[4,2,384,2,384]{4,2,3,1,0:T(8,128)(2,1)} %fusion.1) | data formatting | bytes 9437184 | tf_op jit(solution)/shard_map/reshape;reshape | solution.py:95
  286.7 9.4 %copy.52 = bf16[4,2,384,2,384]{4,3,2,1,0:T(2,128)(2,1)} copy(bf16[4,2,384,2,384]{4,2,3,1,0:T(8,128)(2,1)} %fusion.1) | data formatting | bytes 9437184 | tf_op jit(solution)/shard_map/convert_element_type | solution.py:60
  296.1 11.4 %reshape.94 = bf16[4,768,768]{2,1,0:T(8,128)(2,1)} reshape(bf16[4,2,384,2,384]{4,3,2,1,0:T(2,128)(2,1)} %copy.52) | data formatting | bytes 9437184 | tf_op jit(solution)/shard_map/reshape | solution.py:60
  307.5 2.6 convolution_bitcast_fusion.2
  310.0 2.2 reshape_reshape_reshape.3
  312.2 0.0 all-reduce.11.cloned.1.call-update
  312.3 0.2 all-reduce.13.cloned.1.call-start
  312.5 4.0 convolution_bitcast_fusion.1
  316.5 9.7 %fusion.3 = f32[288,768,16]{1,2,0:T(8,128)} fusion(f32[288,4,768]{2,0,1:T(8,128)S(1)} %convolution_bitcast_fusion.1, s32[4]{0:T(128)S(1)} %copy-done.4), kind=kOutput, calls=%fused_computation.11 | convolution fusion | flops 169869376 | bytes 17694736 | tf_op jit(solution)/shard_map/sk,psx->pkx/dot_general | solution.py:103
  326.2 3.3 convolution_bitcast_fusion
  329.5 25.9 %all-reduce.11.cloned.1.call-done = f32[128,3,384]{2,1,0:T(4,128)} async-done(((f32[128,3,384]{2,1,0:T(4,128)}), f32[128,3,384]{2,1,0:T(4,128)}) %all-reduce.11.cloned.1.call-update) | async-done | bytes 589840
  355.4 1.6 constant_dynamic-slice_fusion.2
  357.0 0.0 reduce-scatter.4.cloned.1.call-start
  357.1 15.3 %add_bitcast_fusion = f32[288,16,768]{2,1,0:T(8,128)} fusion(f32[288,768,16]{1,2,0:T(8,128)} %fusion.3, f32[288,4,768]{2,0,1:T(8,128)} %convolution_bitcast_fusion, s32[4]{0:T(128)S(1)} %copy-done.6), kind=kOutput, calls=%fused_computation.6 | convolution fusion | flops 173408320 | bytes 31850512 | tf_op jit(solution)/shard_map/sk,psx->pkx/dot_general | solution.py:105
  372.4 18.3 %copy.55 = f32[288,16,768]{2,0,1:T(8,128)} copy(f32[288,16,768]{2,1,0:T(8,128)} %add_bitcast_fusion) | data formatting | bytes 28311552 | tf_op jit(solution)/shard_map/add | solution.py:103
  390.7 0.6 copy-done.9
  391.3 0.6 dynamic-slice.8
  391.9 0.6 dynamic-slice.6
  392.5 0.6 dynamic-slice.4
  394.4 5.8 %all-reduce.13.cloned.1.call-done = f32[32,3,384]{2,1,0:T(4,128)} async-done(((f32[32,3,384]{2,1,0:T(4,128)}), f32[32,3,384]{2,1,0:T(4,128)}) %all-reduce.13.cloned.1.call-update) | async-done | bytes 147472
  400.2 0.8 constant_dynamic-slice_fusion.1
  401.0 14.0 %all-reduce.3 = f32[8,3,384]{2,1,0:T(4,128)S(1)} all-reduce(f32[8,3,384]{2,1,0:T(4,128)S(1)} %constant_dynamic-slice_fusion.1), channel_id=8, replica_groups=mesh['orow_0'=4,'orow_1'=4,'ocol_0'=4,'ocol_1'=2] {'ocol_0'}, use_global_device_ids=true, to_apply=%region_4.6.clone | all-reduce | flops 9216 | bytes 73728
  415.0 9.2 %all-reduce.4 = f32[2,3,384]{2,1,0:T(4,128)S(1)} all-reduce(f32[2,3,384]{2,1,0:T(4,128)S(1)} %constant_dynamic-slice_fusion), channel_id=9, replica_groups=mesh['orow_0'=4,'orow_1'=4,'ocol_0'=4,'ocol_1'=2] {'ocol_1'}, use_global_device_ids=true, to_apply=%region_5.7.clone | all-reduce | flops 2304 | bytes 18432
  424.3 0.6 constant_dynamic-slice_fusion.3
  424.9 1.8 all_gather.25
  426.7 10.1 %all-gather = f32[8,3,384]{2,1,0:T(4,128)S(1)} all-gather(f32[2,3,384]{2,1,0:T(4,128)S(1)} %all_gather.25), channel_id=2, replica_groups=mesh['orow_0'=4,'orow_1'=4,'ocol_0'=4,'ocol_1'=2] {'ocol_0'}, dimensions={0}, use_global_device_ids=true | all-gather | bytes 46080 | tf_op jit(solution)/shard_map/all_gather | solution.py:32
  436.9 11.4 %all-gather.1 = f32[16,2,3,384]{3,1,2,0:T(2,128)S(1)} all-gather(f32[4,2,3,384]{3,1,2,0:T(2,128)S(1)} %copy.58), channel_id=3, replica_groups=mesh['orow_0'=4,'orow_1'=4,'ocol_0'=4,'ocol_1'=2] {'orow_1'}, dimensions={0}, use_global_device_ids=true | all-gather | bytes 184320 | tf_op jit(solution)/shard_map/all_gather | solution.py:32
  448.3 14.9 %all-gather.2 = f32[16,4,2,3,384]{4,1,3,2,0:T(4,128)S(1)} all-gather(f32[4,4,2,3,384]{4,1,3,2,0:T(4,128)S(1)} %copy.59), channel_id=4, replica_groups=mesh['orow_0'=4,'orow_1'=4,'ocol_0'=4,'ocol_1'=2] {'orow_0'}, dimensions={0}, use_global_device_ids=true | all-gather | bytes 737280 | tf_op jit(solution)/shard_map/all_gather | solution.py:32
  463.1 0.1 copy_multiply_fusion
  463.3 0.3 copy.61
  463.6 1.1 div.14
  464.7 46.0 %reduce-scatter.4.cloned.1.call-done = f32[288,1,768]{2,0,1:T(8,128)} async-done(((f32[288,16,768]{2,0,1:T(8,128)}), f32[288,1,768]{2,0,1:T(8,128)}) %reduce-scatter.4.cloned.1.call-update) | async-done | bytes 884752
  510.7 2.6 reshape.95
  (37 shorter events, 0.2 us)
Async XLA Ops:
  7.2 4.0 copy-start
  7.2 72.1 %all-gather.5.cloned.1.call-start = ((), (), s32[]{:S(2)}) async-start(), calls=%async_computation.1 | async-start | bytes 7520256 | tf_op jit(solution)/shard_map/all_gather | solution.py:74
  11.0 249.8 %all-reduce.9.cloned.1.call-start = ((), (), s32[]{:S(2)}) async-start(), calls=%async_computation.2 | async-start | bytes 18874368 | tf_op jit(solution)/shard_map/psum | solution.py:90
  11.8 76.0 %copy-start.3 = (s32[4]{0:T(128)}, s32[4]{0:T(128)S(1)}, u32[]{:S(2)}) copy-start(s32[4]{0:T(128)S(1)} %gather_fusion.1) | copy-start | bytes 52
  13.1 74.7 %copy-start.5 = (s32[4]{0:T(128)}, s32[4]{0:T(128)S(1)}, u32[]{:S(2)}) copy-start(s32[4]{0:T(128)S(1)} %gather_fusion) | copy-start | bytes 52
  147.3 208.0 %all-reduce.11.cloned.1.call-start = ((), (), s32[]{:S(2)}) async-start(), calls=%async_computation.3 | async-start | bytes 1572864
  157.6 112.8 %copy-start.2 = (f32[384]{0:T(512)S(1)}, f32[384]{0:T(512)}, u32[]{:S(2)}) copy-start(f32[384]{0:T(512)} %param.11) | copy-start | bytes 4612
  312.3 4.2 copy-start.4
  312.3 87.9 %all-reduce.13.cloned.1.call-start = ((), (), s32[]{:S(2)}) async-start(), calls=%async_computation.4 | async-start | bytes 393216
  312.5 13.7 %slice-start = ((s8[4718592]{0:T(1024)(128)(4,1)}), s8[524288]{0:T(1024)(128)(4,1)S(1)}, s32[]{:S(2)}) async-start(s8[4718592]{0:T(1024)(128)(4,1)} %bitcast.58), calls=%async_computation.6 | async-start | bytes 1048576
  316.5 9.7 %slice-start.1 = ((s8[4718592]{0:T(1024)(128)(4,1)}), s8[4194304]{0:T(1024)(128)(4,1)S(1)}, s32[]{:S(2)}) async-start(s8[4718592]{0:T(1024)(128)(4,1)} %bitcast.58), calls=%async_computation.7 | async-start | bytes 8388608
  326.2 30.9 %copy-start.6 = (s32[4]{0:T(128)S(1)}, s32[4]{0:T(128)}, u32[]{:S(2)}) copy-start(s32[4]{0:T(128)} %copy-done.5) | copy-start | bytes 52
  357.0 153.6 %reduce-scatter.4.cloned.1.call-start = ((), (), s32[]{:S(2)}) async-start(), calls=%async_computation.5 | async-start | bytes 15040512
  390.7 0.7 copy-start.9
  390.7 1.2 copy-start.8
  390.7 1.9 copy-start.7
  391.3 121.9 %copy-start.1 = (s32[64,1]{0,1:T(1,128)S(1)}, s32[64,1]{0,1:T(1,128)}, u32[]{:S(2)}) copy-start(s32[64,1]{0,1:T(1,128)} %param.12) | copy-start | bytes 772
Sparse Core Ops, SparseCore 0:
  11.2 68.0 all-gather.4
  147.5 113.3 all-reduce.8
  312.4 42.9 all-reduce.10
  358.1 42.0 all-reduce.12
  403.6 107.0 reduce-scatter.3
where the time goes:
time: 529 us; the launch traced here: 520 us
  waiting for transfers between devices  247 us (47%)
  local copies, waits for them, and re-layouts  138 us (26%)
  blocking collectives  61.5 us (12%)
  matrix products  40 us (8%)
  other arithmetic  16.9 us (3%)
  between operations  16.2 us (3%)
    psum x1, waiting for transfers between devices, local(): k_total = lax.psum(k_partial, OCOL)  103 us
    unnamed x8, waiting for transfers between devices  77.7 us
    all_gather x1, waiting for transfers between devices, local(): gathered = lax.all_gather(masked, OROW, axis=1, tiled=True)  66.1 us
    all_gather x4, blocking collectives, gather_in_order(): pieces = lax.all_gather(pieces, axes[k])  38.2 us
    reshape x2, local copies, waits for them, and re-layouts, make_amplitudes(): k_grid = k_total.reshape(slots, orbitals, virtuals, orbitals, virtuals)  27.3 us
    unnamed x2, blocking collectives  23.3 us
    reshape x2, local copies, waits for them, and re-layouts, local(): flat_blocks = gathered.reshape(aux_local, block_total, span)  19.6 us
    add x1, local copies, waits for them, and re-layouts, local(): jnp.einsum('sk,psx->pkx', i_onehot, gamma_i, precision=lax.Precision.HIGH...  18.3 us
  transfers between devices with their start and end apart: 5, of which 5 were waited for; matrix products, arithmetic and copies ran while one was open for 13% of the time, Pallas kernels for 0%

commit v1 on v0

--- a/solution.py
+++ b/solution.py
@@ -71,7 +71,9 @@
     my_col = lax.axis_index(OCOL)
     active = jnp.arange(orbitals) < occ_count[my_row]
     masked = integrals * active.astype(jnp.bfloat16)[None, :, None]
-    gathered = lax.all_gather(masked, OROW, axis=1, tiled=True)
+    gathered = jnp.concatenate(
+        lax.all_to_all(jnp.stack([masked] * lax.axis_size(OROW)), OROW, 0, 0), axis=1
+    )
     flat_blocks = gathered.reshape(aux_local, block_total, span)
     first_list = task_iblock[:, 0]
     task_total = first_list.shape[0]

time: 529 us -> 565 us (1.068)
  waiting for transfers between devices: 247 us -> 285 us
  starting transfers between devices: 0.84 us -> 9.4 us
  local copies, waits for them, and re-layouts: 138 us -> 130 us
    all_to_all x0 -> x1, waiting for transfers between devices: none -> 103 us  [local(): lax.all_to_all(jnp.stack([masked] * lax.axis_size(OROW)), OROW, 0, 0)]
    all_gather x1 -> x0, waiting for transfers between devices: 66.1 us -> none  [local(): gathered = lax.all_gather(masked, OROW, axis=1, tiled=True)]
    another operation x0 -> x2, local copies, waits for them, and re-layouts: none -> 21.1 us  [the longest x1 16.1 us: local(): flat_blocks = gathered.reshape(aux_local, block_total, span)]
    reshape x2 -> x0, local copies, waits for them, and re-layouts: 19.6 us -> none  [local(): flat_blocks = gathered.reshape(aux_local, block_total, span)]
    all_to_all x0 -> x1, starting transfers between devices: none -> 8.59 us  [local(): lax.all_to_all(jnp.stack([masked] * lax.axis_size(OROW)), OROW, 0, 0)]
    all_gather x1 -> x0, local copies, waits for them, and re-layouts: 8.54 us -> none  [local(): gathered = lax.all_gather(masked, OROW, axis=1, tiled=True)]
    unnamed x8 -> x7, waiting for transfers between devices: 77.7 us -> 78 us
  transfers between devices with their start and end apart: 5 -> 5, of which waited for: 5 -> 5; matrix products, arithmetic and copies ran while one was open for 13% -> 12% of each run, Pallas kernels for 0% -> 0%
where the time goes in v1:
time: 565 us; the launch traced here: 559 us
  waiting for transfers between devices  285 us (50%)
  local copies, waits for them, and re-layouts  130 us (23%)
  blocking collectives  61.5 us (11%)
  matrix products  40 us (7%)
  other arithmetic  16.4 us (3%)
  between operations  16.2 us (3%)
  starting transfers between devices  9.4 us (2%)
    psum x1, waiting for transfers between devices, local(): k_total = lax.psum(k_partial, OCOL)  105 us
    all_to_all x1, waiting for transfers between devices, local(): lax.all_to_all(jnp.stack([masked] * lax.axis_size(OROW)), OROW, 0, 0)  103 us
    unnamed x7, waiting for transfers between devices  78 us
    all_gather x4, blocking collectives, gather_in_order(): pieces = lax.all_gather(pieces, axes[k])  38.2 us
    reshape x2, local copies, waits for them, and re-layouts, make_amplitudes(): k_grid = k_total.reshape(slots, orbitals, virtuals, orbitals, virtuals)  27.3 us
    unnamed x2, blocking collectives  23.3 us
    add x1, local copies, waits for them, and re-layouts, local(): jnp.einsum('sk,psx->pkx', i_onehot, gamma_i, precision=lax.Precision.HIGH...  18.3 us
    another operation x1, local copies, waits for them, and re-layouts, local(): flat_blocks = gathered.reshape(aux_local, block_total, span)  16.1 us
  transfers between devices with their start and end apart: 5, of which 5 were waited for; matrix products, arithmetic and copies ran while one was open for 12% of the time, Pallas kernels for 0%

profile of v1, /device:TPU:1, one launch (start us, length us, event | category | flops | bytes accessed | tf_op | source)
XLA Modules:
  0.0 558.7 jit_solution(9103877449518423166)
XLA Ops:
  7.2 1.2 dynamic_slice.6
  8.4 0.6 compare_convert_fusion
  9.1 1.5 broadcast_multiply_fusion
  10.5 5.0 stack.2
  15.5 8.6 %all-to-all-start = ((bf16[16,288,2,384]{3,2,1,0:T(2,128)(2,1)}), bf16[16,288,2,384]{3,2,1,0:T(2,128)(2,1)}, u32[]{:S(2)}, u32[]{:S(2)}) async-start(bf16[16,288,2,384]{3,2,1,0:T(2,128)(2,1)} %stack.2), calls=%async_computation | async-start | bytes 14155776 | tf_op jit(solution)/shard_map/all_to_all | solution.py:75
  24.1 0.0 all-reduce.9.cloned.1.call-start
  24.2 0.6 gather_fusion.1
  24.8 0.6 gather_fusion
  25.5 102.6 %all-to-all-done = bf16[16,288,2,384]{3,2,1,0:T(2,128)(2,1)} async-done(((bf16[16,288,2,384]{3,2,1,0:T(2,128)(2,1)}), bf16[16,288,2,384]{3,2,1,0:T(2,128)(2,1)}, u32[]{:S(2)}, u32[]{:S(2)}) %all-to-all-start) | async-done | bytes 7077920 | tf_op jit(solution)/shard_map/all_to_all | solution.py:75
  128.2 16.1 %reshape_reshape.7 = bf16[288,16,768]{2,0,1:T(8,128)(2,1)} reshape(bf16[288,16,2,384]{3,2,0,1:T(2,128)(2,1)} %bitcast.2) | data formatting | bytes 14155776 | tf_op jit(solution)/shard_map/reshape;reshape | solution.py:77
  144.3 3.7 gather_fusion.5
  148.0 3.7 gather_fusion.4
  151.6 5.2 fusion.6
  156.8 12.5 %reshape.94 = f32[4,2,384,2,384]{4,3,2,1,0:T(2,128)} reshape(f32[4,768,768]{2,1,0:T(8,128)} %fusion.6) | data formatting | bytes 18874368 | tf_op jit(solution)/shard_map/reshape | solution.py:51
  169.4 14.8 %copy.31 = f32[4,2,384,2,384]{2,4,3,1,0:T(8,128)} copy(f32[4,2,384,2,384]{4,3,2,1,0:T(2,128)} %reshape.94) | data formatting | bytes 18874368 | tf_op jit(solution)/shard_map/reshape | solution.py:51
  184.2 0.0 all-reduce.9.cloned.1.call-update
  184.2 0.5 all-reduce.11.cloned.1.call-start
  184.7 0.7 reshape.95
  185.5 0.7 fusion.19
  186.1 0.6 pad_clamp_fusion
  186.7 1.3 gather_fusion.3
  188.0 0.6 fusion.18
  188.6 0.6 pad_clamp_fusion.1
  189.2 1.3 gather_fusion.2
  190.4 1.2 dynamic-slice.2
  192.3 0.8 broadcast_add_fusion
  193.1 1.4 broadcast_subtract_fusion
  194.5 104.7 %all-reduce.9.cloned.1.call-done = f32[4,2,384,2,384]{2,4,3,1,0:T(8,128)} async-done(((f32[4,2,384,2,384]{2,4,3,1,0:T(8,128)}), f32[4,2,384,2,384]{2,4,3,1,0:T(8,128)}) %all-reduce.9.cloned.1.call-update) | async-done | bytes 9437200 | tf_op jit(solution)/shard_map/psum | solution.py:92
  299.2 9.6 %copy.32 = f32[4,2,384,2,384]{4,2,3,1,0:T(8,128)} copy(f32[4,2,384,2,384]{2,4,3,1,0:T(8,128)} %all-reduce.9.cloned.1.call-done) | data formatting | bytes 18874368 | tf_op jit(solution)/shard_map/psum | solution.py:92
  308.8 9.6 %fusion.1 = bf16[4,2,384,2,384]{4,2,3,1,0:T(8,128)(2,1)} fusion(f32[4,2,384,2,384]{2,4,3,1,0:T(8,128)} %all-reduce.9.cloned.1.call-done, f32[4,2,384,2,384]{4,2,3,1,0:T(8,128)} %copy.32, f32[384]{0:T(512)S(1)} %copy-done.3, f32[4,2,384,2]{2,3,1,0:T(2,128)} %broadcast_subtract_fusion), kind=kLoop, calls=%fused_computation.9 | loop fusion | flops 11796480 | bytes 23619072 | tf_op jit(solution)/shard_map/convert_element_type | solution.py:60
  318.4 6.7 %copy.44 = bf16[4,2,384,2,384]{2,4,3,0,1:T(8,128)(2,1)} copy(bf16[4,2,384,2,384]{4,2,3,1,0:T(8,128)(2,1)} %fusion.1) | data formatting | bytes 9437184 | tf_op jit(solution)/shard_map/reshape;reshape | solution.py:97
  325.1 9.4 %copy.33 = bf16[4,2,384,2,384]{4,3,2,1,0:T(2,128)(2,1)} copy(bf16[4,2,384,2,384]{4,2,3,1,0:T(8,128)(2,1)} %fusion.1) | data formatting | bytes 9437184 | tf_op jit(solution)/shard_map/convert_element_type | solution.py:60
  334.5 11.4 %reshape.96 = bf16[4,768,768]{2,1,0:T(8,128)(2,1)} reshape(bf16[4,2,384,2,384]{4,3,2,1,0:T(2,128)(2,1)} %copy.33) | data formatting | bytes 9437184 | tf_op jit(solution)/shard_map/reshape | solution.py:60
  345.9 2.6 convolution_bitcast_fusion.2
  348.4 2.2 reshape_reshape_reshape.3
  350.6 0.0 all-reduce.11.cloned.1.call-update
  350.7 0.2 all-reduce.13.cloned.1.call-start
  350.9 4.0 convolution_bitcast_fusion.1
  354.9 9.7 %fusion.3 = f32[288,768,16]{1,2,0:T(8,128)} fusion(f32[288,4,768]{2,0,1:T(8,128)S(1)} %convolution_bitcast_fusion.1, s32[4]{0:T(128)S(1)} %copy-done.5), kind=kOutput, calls=%fused_computation.11 | convolution fusion | flops 169869376 | bytes 17694736 | tf_op jit(solution)/shard_map/sk,psx->pkx/dot_general | solution.py:105
  364.6 3.3 convolution_bitcast_fusion
  367.9 25.9 %all-reduce.11.cloned.1.call-done = f32[128,3,384]{2,1,0:T(4,128)} async-done(((f32[128,3,384]{2,1,0:T(4,128)}), f32[128,3,384]{2,1,0:T(4,128)}) %all-reduce.11.cloned.1.call-update) | async-done | bytes 589840
  393.8 1.6 constant_dynamic-slice_fusion.2
  395.4 0.0 all-reduce.13.cloned.1.call-update
  395.4 0.0 reduce-scatter.4.cloned.1.call-start
  395.5 15.3 %add_bitcast_fusion = f32[288,16,768]{2,1,0:T(8,128)} fusion(f32[288,768,16]{1,2,0:T(8,128)} %fusion.3, f32[288,4,768]{2,0,1:T(8,128)} %convolution_bitcast_fusion, s32[4]{0:T(128)S(1)} %copy-done.7), kind=kOutput, calls=%fused_computation.6 | convolution fusion | flops 173408320 | bytes 31850512 | tf_op jit(solution)/shard_map/sk,psx->pkx/dot_general | solution.py:107
  410.8 18.3 %copy.36 = f32[288,16,768]{2,0,1:T(8,128)} copy(f32[288,16,768]{2,1,0:T(8,128)} %add_bitcast_fusion) | data formatting | bytes 28311552 | tf_op jit(solution)/shard_map/add | solution.py:105
  429.1 0.6 copy-done.10
  429.7 0.6 dynamic-slice.8
  430.3 0.6 dynamic-slice.6
  430.9 0.6 dynamic-slice.4
  432.8 6.0 %all-reduce.13.cloned.1.call-done = f32[32,3,384]{2,1,0:T(4,128)} async-done(((f32[32,3,384]{2,1,0:T(4,128)}), f32[32,3,384]{2,1,0:T(4,128)}) %all-reduce.13.cloned.1.call-update) | async-done | bytes 147472
  438.7 0.8 constant_dynamic-slice_fusion.1
  439.6 14.0 %all-reduce.3 = f32[8,3,384]{2,1,0:T(4,128)S(1)} all-reduce(f32[8,3,384]{2,1,0:T(4,128)S(1)} %constant_dynamic-slice_fusion.1), channel_id=8, replica_groups=mesh['orow_0'=4,'orow_1'=4,'ocol_0'=4,'ocol_1'=2] {'ocol_0'}, use_global_device_ids=true, to_apply=%region_4.6.clone | all-reduce | flops 9216 | bytes 73728
  453.6 9.2 %all-reduce.4 = f32[2,3,384]{2,1,0:T(4,128)S(1)} all-reduce(f32[2,3,384]{2,1,0:T(4,128)S(1)} %constant_dynamic-slice_fusion), channel_id=9, replica_groups=mesh['orow_0'=4,'orow_1'=4,'ocol_0'=4,'ocol_1'=2] {'ocol_1'}, use_global_device_ids=true, to_apply=%region_5.7.clone | all-reduce | flops 2304 | bytes 18432
  462.8 0.6 constant_dynamic-slice_fusion.3
  463.4 1.8 all_gather.21
  465.2 10.1 %all-gather = f32[8,3,384]{2,1,0:T(4,128)S(1)} all-gather(f32[2,3,384]{2,1,0:T(4,128)S(1)} %all_gather.21), channel_id=2, replica_groups=mesh['orow_0'=4,'orow_1'=4,'ocol_0'=4,'ocol_1'=2] {'ocol_0'}, dimensions={0}, use_global_device_ids=true | all-gather | bytes 46080 | tf_op jit(solution)/shard_map/all_gather | solution.py:32
  475.4 11.3 %all-gather.1 = f32[16,2,3,384]{3,1,2,0:T(2,128)S(1)} all-gather(f32[4,2,3,384]{3,1,2,0:T(2,128)S(1)} %copy.39), channel_id=3, replica_groups=mesh['orow_0'=4,'orow_1'=4,'ocol_0'=4,'ocol_1'=2] {'orow_1'}, dimensions={0}, use_global_device_ids=true | all-gather | bytes 184320 | tf_op jit(solution)/shard_map/all_gather | solution.py:32
  486.8 14.9 %all-gather.2 = f32[16,4,2,3,384]{4,1,3,2,0:T(4,128)S(1)} all-gather(f32[4,4,2,3,384]{4,1,3,2,0:T(4,128)S(1)} %copy.40), channel_id=4, replica_groups=mesh['orow_0'=4,'orow_1'=4,'ocol_0'=4,'ocol_1'=2] {'orow_0'}, dimensions={0}, use_global_device_ids=true | all-gather | bytes 737280 | tf_op jit(solution)/shard_map/all_gather | solution.py:32
  501.7 0.1 copy_multiply_fusion
  501.8 0.3 copy.42
  502.2 1.1 div.14
  503.3 46.1 %reduce-scatter.4.cloned.1.call-done = f32[288,1,768]{2,0,1:T(8,128)} async-done(((f32[288,16,768]{2,0,1:T(8,128)}), f32[288,1,768]{2,0,1:T(8,128)}) %reduce-scatter.4.cloned.1.call-update) | async-done | bytes 884752
  549.3 2.6 reshape.97
  (37 shorter events, 0.2 us)
Async XLA Ops:
  7.2 17.0 %copy-start = (s32[64,1]{0,1:T(1,128)S(1)}, s32[64,1]{0,1:T(1,128)}, u32[]{:S(2)}) copy-start(s32[64,1]{0,1:T(1,128)} %param.12) | copy-start | bytes 772
  15.5 9.3 %copy-start.2 = (s32[64]{0:T(128)S(1)}, s32[64]{0:T(128)}, u32[]{:S(2)}) copy-start(s32[64]{0:T(128)} %param.13) | copy-start | bytes 772
  15.5 112.7 %all-to-all-start = ((bf16[16,288,2,384]{3,2,1,0:T(2,128)(2,1)}), bf16[16,288,2,384]{3,2,1,0:T(2,128)(2,1)}, u32[]{:S(2)}, u32[]{:S(2)}) async-start(bf16[16,288,2,384]{3,2,1,0:T(2,128)(2,1)} %stack.2), calls=%async_computation | async-start | bytes 14155776 | tf_op jit(solution)/shard_map/all_to_all | solution.py:75
  24.1 275.1 %all-reduce.9.cloned.1.call-start = ((), (), s32[]{:S(2)}) async-start(), calls=%async_computation.2 | async-start | bytes 18874368 | tf_op jit(solution)/shard_map/psum | solution.py:92
  24.8 119.4 %copy-start.4 = (s32[4]{0:T(128)}, s32[4]{0:T(128)S(1)}, u32[]{:S(2)}) copy-start(s32[4]{0:T(128)S(1)} %gather_fusion.1) | copy-start | bytes 52
  25.5 118.8 %copy-start.6 = (s32[4]{0:T(128)}, s32[4]{0:T(128)S(1)}, u32[]{:S(2)}) copy-start(s32[4]{0:T(128)S(1)} %gather_fusion) | copy-start | bytes 52
  184.2 209.6 %all-reduce.11.cloned.1.call-start = ((), (), s32[]{:S(2)}) async-start(), calls=%async_computation.3 | async-start | bytes 1572864
  194.5 114.3 %copy-start.3 = (f32[384]{0:T(512)S(1)}, f32[384]{0:T(512)}, u32[]{:S(2)}) copy-start(f32[384]{0:T(512)} %param.11) | copy-start | bytes 4612
  350.6 4.2 copy-start.5
  350.7 88.1 %all-reduce.13.cloned.1.call-start = ((), (), s32[]{:S(2)}) async-start(), calls=%async_computation.4 | async-start | bytes 393216
  350.9 13.7 %slice-start = ((s8[4718592]{0:T(1024)(128)(4,1)}), s8[524288]{0:T(1024)(128)(4,1)S(1)}, s32[]{:S(2)}) async-start(s8[4718592]{0:T(1024)(128)(4,1)} %bitcast.61), calls=%async_computation.6 | async-start | bytes 1048576
  354.9 9.7 %slice-start.1 = ((s8[4718592]{0:T(1024)(128)(4,1)}), s8[4194304]{0:T(1024)(128)(4,1)S(1)}, s32[]{:S(2)}) async-start(s8[4718592]{0:T(1024)(128)(4,1)} %bitcast.61), calls=%async_computation.7 | async-start | bytes 8388608
  364.6 30.9 %copy-start.7 = (s32[4]{0:T(128)S(1)}, s32[4]{0:T(128)}, u32[]{:S(2)}) copy-start(s32[4]{0:T(128)} %copy-done.6) | copy-start | bytes 52
  395.4 153.9 %reduce-scatter.4.cloned.1.call-start = ((), (), s32[]{:S(2)}) async-start(), calls=%async_computation.5 | async-start | bytes 15040512
  429.1 0.7 copy-start.10
  429.1 1.2 copy-start.9
  429.1 1.9 copy-start.8
  429.7 122.2 %copy-start.1 = (s32[64,1]{0,1:T(1,128)S(1)}, s32[64,1]{0,1:T(1,128)}, u32[]{:S(2)}) copy-start(s32[64,1]{0,1:T(1,128)} %param.12) | copy-start | bytes 772
Sparse Core Ops, SparseCore 0:
  184.3 114.8 all-reduce.8
  350.8 42.9 all-reduce.10
  396.7 42.0 all-reduce.12
  442.1 107.1 reduce-scatter.3
